TPU v7x, 32 devices: a whole 2x2x4 slice. The times are simulated.
32 devices in a mesh: group: 1, ctx: 32 (over z, y, x, core).
Axes of the slice: x: 2, y: 2, z: 4, core: 2. Of those that a mesh axis runs over, the one named last changes fastest.
Arguments:
- history: bfloat16 [2, 1024, 8192], P('group', 'ctx'), may hold values from -6 to 6
- lengths: int32 [2], P('group'), may hold values from 256 to 1024
- token_ids: int32 [2, 512], P('group'), may hold values from 0 to 511
- embed: bfloat16 [512, 8192], P('ctx'), may hold values from -6 to 6
- residue: float32 [16, 8192], replicated, may hold values from -0.046875 to 0.046875
- decay: float32 [16, 8192], replicated, may hold values from 0.1 to 400
- skip: float32 [8192], replicated, may hold values from 0.5 to 1.5
Outputs:
- mixed: bfloat16 [2, 512, 8192], P('group', 'ctx')
Inputs may be any that keep to these rules, and one draw needn't show every extreme that they name: `lengths`: history positions at or past a sequence's length are ignored.
All inputs are finite; a program needn't handle non-finite values.
Results may differ from a plain program's by a relative error of at most 0.0005.
Values may be sent and summed in bfloat16 or wider, within the bound.
No kernel may reach another device: no remote copies, remote signals or barrier semaphores. Data moves between devices by JAX's collectives and lax.ppermute only.
A program may use at most 128 MiB of HBM per device.

v0:
```python
import jax
import jax.numpy as jnp
from jax import lax
from jax.sharding import PartitionSpec as P

STEP_LEN = 128


def body(history, lengths, token_ids, embed, residue, decay, skip):
    devices = lax.axis_size("ctx")
    myself = lax.axis_index("ctx")
    seqs, tile, width = history.shape
    narrow = width // devices
    total_len = tile * devices
    rates = decay / total_len
    start = myself * tile
    places = start + jnp.arange(tile, dtype=jnp.int32)
    inside = places[None, :] < lengths[:, None]
    masked = jnp.where(inside[:, :, None], history, jnp.zeros_like(history))
    ends = start + tile
    lift = jnp.maximum(lengths - ends, -tile).astype(jnp.float32)
    spans = (ends - places).astype(jnp.float32)

    def per_mode(rate_row):
        local = jnp.exp(-rate_row[None, :] * spans[:, None])
        part = jnp.sum(local[None, :, :] * masked, axis=1)
        return part * jnp.exp(-rate_row[None, :] * lift[:, None])

    partial_states = lax.map(per_mode, rates)
    summed = lax.psum(partial_states, "ctx")
    mine = lax.dynamic_slice_in_dim(summed, myself * narrow, narrow, 2)
    full_table = lax.all_gather(embed, "ctx", axis=0, tiled=True)
    columns = lax.dynamic_slice_in_dim(full_table, myself * narrow, narrow, 1)
    vocab = columns.shape[0]
    onehot = (token_ids[:, :, None] == jnp.arange(vocab, dtype=jnp.int32)[None, None, :]).astype(
        jnp.bfloat16
    )
    fresh = jnp.einsum("btv,vc->btc", onehot, columns, preferred_element_type=jnp.float32).astype(
        jnp.bfloat16
    )
    my_rates = lax.dynamic_slice_in_dim(rates, myself * narrow, narrow, 1)
    my_residue = lax.dynamic_slice_in_dim(residue, myself * narrow, narrow, 1)
    my_skip = lax.dynamic_slice_in_dim(skip, myself * narrow, narrow, 0)
    generated = token_ids.shape[1]
    steps_count = generated // STEP_LEN
    times = jnp.arange(generated, dtype=jnp.int32).astype(jnp.float32)
    decays = jnp.exp(-my_rates[:, None, :] * times[None, :, None])
    weighted = my_residue[:, None, :] * decays
    history_part = jnp.einsum("ktc,kbc->btc", weighted, mine, precision=lax.Precision.HIGHEST)
    fresh_wide = fresh.astype(jnp.float32)
    pieces = fresh_wide.reshape(seqs, steps_count, STEP_LEN, narrow)
    ladder = jnp.arange(STEP_LEN, dtype=jnp.int32)
    offset = ladder[:, None] - ladder[None, :]
    below = (offset >= 0)[:, :, None]
    gaps = jnp.maximum(offset, 0).astype(jnp.float32)

    def add_mode(index, block):
        rate_row = my_rates[index]
        return block + my_residue[index][None, None, :] * jnp.exp(
            -rate_row[None, None, :] * gaps[:, :, None]
        )

    toeplitz = lax.fori_loop(
        0, my_rates.shape[0], add_mode, jnp.zeros((STEP_LEN, STEP_LEN, narrow), jnp.float32)
    )
    toeplitz = jnp.where(below, toeplitz, 0.0)
    near_part = jnp.einsum("tsc,bjsc->bjtc", toeplitz, pieces, precision=lax.Precision.HIGHEST)
    ladder_f = ladder.astype(jnp.float32)
    into_step = my_residue[:, None, :] * jnp.exp(-my_rates[:, None, :] * ladder_f[None, :, None])
    out_of_step = jnp.exp(-my_rates[:, None, :] * (STEP_LEN - ladder_f)[None, :, None])
    step_decay = jnp.exp(-my_rates * STEP_LEN)
    carry = jnp.zeros((my_rates.shape[0], seqs, narrow), jnp.float32)
    far_blocks = []
    for index in range(steps_count):
        far_blocks.append(
            jnp.einsum("kuc,kbc->buc", into_step, carry, precision=lax.Precision.HIGHEST)
        )
        step_state = jnp.einsum(
            "ksc,bsc->kbc", out_of_step, pieces[:, index], precision=lax.Precision.HIGHEST
        )
        carry = step_decay[:, None, :] * carry + step_state
    far_part = jnp.stack(far_blocks, axis=1)
    conv_part = (near_part + far_part).reshape(seqs, generated, narrow)
    mixed = (history_part + conv_part + my_skip[None, None, :] * fresh_wide).astype(jnp.bfloat16)
    return lax.all_to_all(mixed, "ctx", split_axis=1, concat_axis=2, tiled=True)


def solution(mesh):
    placed = (P("group", "ctx", None), P("group"), P("group", None), P("ctx", None), P(), P(), P())
    return jax.shard_map(
        body, mesh=mesh, in_specs=placed, out_specs=P("group", "ctx", None), check_vma=False
    )
```

profile of v0, /device:TPU:0, one launch (start us, length us, event | category | flops | bytes accessed | tf_op | source)
XLA Modules:
  0.0 337.1 jit_solution(2049569387925838529)
XLA Ops:
  6.5 0.7 all-gather.2.cloned.1.call-update
  7.3 1.1 broadcast_multiply_fusion
  8.4 0.7 broadcast_compare_fusion
  9.1 0.7 maximum_convert_fusion.1
  9.8 1.4 broadcast_select_fusion
  11.2 12.9 %while.25 = (s32[]{:T(128)}, f32[16,2,8192]{2,1,0:T(2,128)S(1)}, f32[16,8192]{1,0:T(8,128)S(1)}, bf16[2,32,8192]{2,1,0:T(8,128)(2,1)S(1)}, f32[2]{0:T(128)S(1)}, /*index=5*/s32[]{:T(128)}, s32[]{:T(128)}, s32[]{:T(128)}) while((s32[]{:T(128)}, f32[16,2,8192]{2,1,0:T(2,128)S(1)}, f32[16,8192]{1,0:T(8,128)S(1)}, ...), condition=%wide.region_2.3_spmd.clone, body=%wide.region_0.2_spmd.clone.sunk | while | flops 1859682 | bytes 3474285 | solution.py:29
  11.2 0.2 multiply_exponential_fusion.19
  11.5 0.4 multiply_reduce_fusion.2
  12.3 0.4 multiply_reduce_fusion.2
  12.9 0.2 multiply_exponential_fusion.19
  13.1 0.4 multiply_reduce_fusion.2
  13.7 0.2 multiply_exponential_fusion.19
  13.9 0.4 multiply_reduce_fusion.2
  14.5 0.2 multiply_exponential_fusion.19
  14.7 0.4 multiply_reduce_fusion.2
  15.5 0.4 multiply_reduce_fusion.2
  16.3 0.4 multiply_reduce_fusion.2
  17.1 0.4 multiply_reduce_fusion.2
  17.9 0.4 multiply_reduce_fusion.2
  18.7 0.4 multiply_reduce_fusion.2
  19.5 0.4 multiply_reduce_fusion.2
  20.4 0.4 multiply_reduce_fusion.2
  21.2 0.4 multiply_reduce_fusion.2
  22.0 0.4 multiply_reduce_fusion.2
  22.8 0.4 multiply_reduce_fusion.2
  23.6 0.4 multiply_reduce_fusion.2
  24.1 7.8 %copy.64 = f32[16,2,8192]{0,1,2:T(2,128)} copy(f32[16,2,8192]{2,1,0:T(2,128)S(1)} %get-tuple-element.131) | data formatting | bytes 2097152 | tf_op jit(solution)/shard_map/while | solution.py:29
  32.1 196.6 %while.26 = (s32[]{:T(128)}, f32[128,128,256]{2,1,0:T(8,128)}, f32[16,256]{1,0:T(8,128)S(1)}, f32[16,256]{1,0:T(8,128)S(1)}, s32[]{:T(128)}, /*index=5*/s32[]{:T(128)}) while((s32[]{:T(128)}, f32[128,128,256]{2,1,0:T(8,128)}, f32[16,256]{1,0:T(8,128)S(1)}, f32[16,256]{1,0:T(8,128)S(1)}, s32[]{:T(128)}, /*index=5*/s32[]{:T(128)}) %tuple.55), condition=%wide.region_5.6_spmd.clone, body=%wide.region_4.5_spmd.clone.sunk | while | flops 16826628 | bytes 33691736 | solution.py:63
  32.2 7.0 %select_add_fusion.2 = f32[128,128,256]{2,1,0:T(8,128)} fusion(f32[128,128,256]{2,1,0:T(8,128)} %get-tuple-element.278, f32[128,128]{1,0:T(8,128)S(1)} %maximum_convert_fusion.3, f32[256]{0:T(256)S(1)} %bitcast.86, f32[256]{0:T(256)S(1)} %bitcast.87, pred[]{:T(512)S(6)} %compare.3), kind=kLoop, calls=%fused_computation.8.clone.1 | loop fusion | flops 16777216 | bytes 33622016 | tf_op jit(solution)/shard_map/while/body/eval_jaxpr/add | solution.py:59
  39.3 12.5 %select_add_fusion.2 = f32[128,128,256]{2,1,0:T(8,128)} fusion(f32[128,128,256]{2,1,0:T(8,128)} %get-tuple-element.278, f32[128,128]{1,0:T(8,128)S(1)} %maximum_convert_fusion.3, f32[256]{0:T(256)S(1)} %bitcast.86, f32[256]{0:T(256)S(1)} %bitcast.87, pred[]{:T(512)S(6)} %compare.3), kind=kLoop, calls=%fused_computation.8.clone.1 | loop fusion | flops 16777216 | bytes 33622016 | tf_op jit(solution)/shard_map/while/body/eval_jaxpr/add | solution.py:59
  51.8 12.8 %select_add_fusion.2 = f32[128,128,256]{2,1,0:T(8,128)} fusion(f32[128,128,256]{2,1,0:T(8,128)} %get-tuple-element.278, f32[128,128]{1,0:T(8,128)S(1)} %maximum_convert_fusion.3, f32[256]{0:T(256)S(1)} %bitcast.86, f32[256]{0:T(256)S(1)} %bitcast.87, pred[]{:T(512)S(6)} %compare.3), kind=kLoop, calls=%fused_computation.8.clone.1 | loop fusion | flops 16777216 | bytes 33622016 | tf_op jit(solution)/shard_map/while/body/eval_jaxpr/add | solution.py:59
  64.6 12.5 %select_add_fusion.2 = f32[128,128,256]{2,1,0:T(8,128)} fusion(f32[128,128,256]{2,1,0:T(8,128)} %get-tuple-element.278, f32[128,128]{1,0:T(8,128)S(1)} %maximum_convert_fusion.3, f32[256]{0:T(256)S(1)} %bitcast.86, f32[256]{0:T(256)S(1)} %bitcast.87, pred[]{:T(512)S(6)} %compare.3), kind=kLoop, calls=%fused_computation.8.clone.1 | loop fusion | flops 16777216 | bytes 33622016 | tf_op jit(solution)/shard_map/while/body/eval_jaxpr/add | solution.py:59
  77.2 12.7 %select_add_fusion.2 = f32[128,128,256]{2,1,0:T(8,128)} fusion(f32[128,128,256]{2,1,0:T(8,128)} %get-tuple-element.278, f32[128,128]{1,0:T(8,128)S(1)} %maximum_convert_fusion.3, f32[256]{0:T(256)S(1)} %bitcast.86, f32[256]{0:T(256)S(1)} %bitcast.87, pred[]{:T(512)S(6)} %compare.3), kind=kLoop, calls=%fused_computation.8.clone.1 | loop fusion | flops 16777216 | bytes 33622016 | tf_op jit(solution)/shard_map/while/body/eval_jaxpr/add | solution.py:59
  89.9 12.8 %select_add_fusion.2 = f32[128,128,256]{2,1,0:T(8,128)} fusion(f32[128,128,256]{2,1,0:T(8,128)} %get-tuple-element.278, f32[128,128]{1,0:T(8,128)S(1)} %maximum_convert_fusion.3, f32[256]{0:T(256)S(1)} %bitcast.86, f32[256]{0:T(256)S(1)} %bitcast.87, pred[]{:T(512)S(6)} %compare.3), kind=kLoop, calls=%fused_computation.8.clone.1 | loop fusion | flops 16777216 | bytes 33622016 | tf_op jit(solution)/shard_map/while/body/eval_jaxpr/add | solution.py:59
  102.7 12.6 %select_add_fusion.2 = f32[128,128,256]{2,1,0:T(8,128)} fusion(f32[128,128,256]{2,1,0:T(8,128)} %get-tuple-element.278, f32[128,128]{1,0:T(8,128)S(1)} %maximum_convert_fusion.3, f32[256]{0:T(256)S(1)} %bitcast.86, f32[256]{0:T(256)S(1)} %bitcast.87, pred[]{:T(512)S(6)} %compare.3), kind=kLoop, calls=%fused_computation.8.clone.1 | loop fusion | flops 16777216 | bytes 33622016 | tf_op jit(solution)/shard_map/while/body/eval_jaxpr/add | solution.py:59
  115.4 12.7 %select_add_fusion.2 = f32[128,128,256]{2,1,0:T(8,128)} fusion(f32[128,128,256]{2,1,0:T(8,128)} %get-tuple-element.278, f32[128,128]{1,0:T(8,128)S(1)} %maximum_convert_fusion.3, f32[256]{0:T(256)S(1)} %bitcast.86, f32[256]{0:T(256)S(1)} %bitcast.87, pred[]{:T(512)S(6)} %compare.3), kind=kLoop, calls=%fused_computation.8.clone.1 | loop fusion | flops 16777216 | bytes 33622016 | tf_op jit(solution)/shard_map/while/body/eval_jaxpr/add | solution.py:59
  128.1 12.6 %select_add_fusion.2 = f32[128,128,256]{2,1,0:T(8,128)} fusion(f32[128,128,256]{2,1,0:T(8,128)} %get-tuple-element.278, f32[128,128]{1,0:T(8,128)S(1)} %maximum_convert_fusion.3, f32[256]{0:T(256)S(1)} %bitcast.86, f32[256]{0:T(256)S(1)} %bitcast.87, pred[]{:T(512)S(6)} %compare.3), kind=kLoop, calls=%fused_computation.8.clone.1 | loop fusion | flops 16777216 | bytes 33622016 | tf_op jit(solution)/shard_map/while/body/eval_jaxpr/add | solution.py:59
  140.8 12.5 %select_add_fusion.2 = f32[128,128,256]{2,1,0:T(8,128)} fusion(f32[128,128,256]{2,1,0:T(8,128)} %get-tuple-element.278, f32[128,128]{1,0:T(8,128)S(1)} %maximum_convert_fusion.3, f32[256]{0:T(256)S(1)} %bitcast.86, f32[256]{0:T(256)S(1)} %bitcast.87, pred[]{:T(512)S(6)} %compare.3), kind=kLoop, calls=%fused_computation.8.clone.1 | loop fusion | flops 16777216 | bytes 33622016 | tf_op jit(solution)/shard_map/while/body/eval_jaxpr/add | solution.py:59
  153.4 12.5 %select_add_fusion.2 = f32[128,128,256]{2,1,0:T(8,128)} fusion(f32[128,128,256]{2,1,0:T(8,128)} %get-tuple-element.278, f32[128,128]{1,0:T(8,128)S(1)} %maximum_convert_fusion.3, f32[256]{0:T(256)S(1)} %bitcast.86, f32[256]{0:T(256)S(1)} %bitcast.87, pred[]{:T(512)S(6)} %compare.3), kind=kLoop, calls=%fused_computation.8.clone.1 | loop fusion | flops 16777216 | bytes 33622016 | tf_op jit(solution)/shard_map/while/body/eval_jaxpr/add | solution.py:59
  166.0 12.5 %select_add_fusion.2 = f32[128,128,256]{2,1,0:T(8,128)} fusion(f32[128,128,256]{2,1,0:T(8,128)} %get-tuple-element.278, f32[128,128]{1,0:T(8,128)S(1)} %maximum_convert_fusion.3, f32[256]{0:T(256)S(1)} %bitcast.86, f32[256]{0:T(256)S(1)} %bitcast.87, pred[]{:T(512)S(6)} %compare.3), kind=kLoop, calls=%fused_computation.8.clone.1 | loop fusion | flops 16777216 | bytes 33622016 | tf_op jit(solution)/shard_map/while/body/eval_jaxpr/add | solution.py:59
  178.5 12.6 %select_add_fusion.2 = f32[128,128,256]{2,1,0:T(8,128)} fusion(f32[128,128,256]{2,1,0:T(8,128)} %get-tuple-element.278, f32[128,128]{1,0:T(8,128)S(1)} %maximum_convert_fusion.3, f32[256]{0:T(256)S(1)} %bitcast.86, f32[256]{0:T(256)S(1)} %bitcast.87, pred[]{:T(512)S(6)} %compare.3), kind=kLoop, calls=%fused_computation.8.clone.1 | loop fusion | flops 16777216 | bytes 33622016 | tf_op jit(solution)/shard_map/while/body/eval_jaxpr/add | solution.py:59
  191.1 12.4 %select_add_fusion.2 = f32[128,128,256]{2,1,0:T(8,128)} fusion(f32[128,128,256]{2,1,0:T(8,128)} %get-tuple-element.278, f32[128,128]{1,0:T(8,128)S(1)} %maximum_convert_fusion.3, f32[256]{0:T(256)S(1)} %bitcast.86, f32[256]{0:T(256)S(1)} %bitcast.87, pred[]{:T(512)S(6)} %compare.3), kind=kLoop, calls=%fused_computation.8.clone.1 | loop fusion | flops 16777216 | bytes 33622016 | tf_op jit(solution)/shard_map/while/body/eval_jaxpr/add | solution.py:59
  203.6 12.7 %select_add_fusion.2 = f32[128,128,256]{2,1,0:T(8,128)} fusion(f32[128,128,256]{2,1,0:T(8,128)} %get-tuple-element.278, f32[128,128]{1,0:T(8,128)S(1)} %maximum_convert_fusion.3, f32[256]{0:T(256)S(1)} %bitcast.86, f32[256]{0:T(256)S(1)} %bitcast.87, pred[]{:T(512)S(6)} %compare.3), kind=kLoop, calls=%fused_computation.8.clone.1 | loop fusion | flops 16777216 | bytes 33622016 | tf_op jit(solution)/shard_map/while/body/eval_jaxpr/add | solution.py:59
  216.3 12.5 %select_add_fusion.2 = f32[128,128,256]{2,1,0:T(8,128)} fusion(f32[128,128,256]{2,1,0:T(8,128)} %get-tuple-element.278, f32[128,128]{1,0:T(8,128)S(1)} %maximum_convert_fusion.3, f32[256]{0:T(256)S(1)} %bitcast.86, f32[256]{0:T(256)S(1)} %bitcast.87, pred[]{:T(512)S(6)} %compare.3), kind=kLoop, calls=%fused_computation.8.clone.1 | loop fusion | flops 16777216 | bytes 33622016 | tf_op jit(solution)/shard_map/while/body/eval_jaxpr/add | solution.py:59
  228.7 13.4 %select_bitcast_fusion = f32[128,128,256,1]{2,1,0,3:T(8,128)} fusion(f32[128,128,256]{2,1,0:T(8,128)} %get-tuple-element.132, pred[128,128]{1,0:T(8,128)(4,1)S(1)} %subtract_compare_fusion), kind=kLoop, calls=%fused_computation.12 | loop fusion | flops 4194304 | bytes 33570816 | tf_op jit(solution)/shard_map/jit(_where)/select_n | solution.py:66
  242.2 18.1 %copy.80 = f32[128,128,256,1]{1,0,3,2:T(8,128)} copy(f32[128,128,256,1]{2,1,0,3:T(8,128)} %select_bitcast_fusion) | data formatting | bytes 33554432 | tf_op jit(solution)/shard_map/jit(_where)/select_n | solution.py:66
  260.6 0.8 dynamic_slice.37
  261.3 2.8 fusion.18
  264.2 1.5 fusion.19
  265.7 0.5 copy.67
  266.2 0.3 reshape.164
  266.5 0.6 fusion.65
  267.3 2.2 fusion.34
  269.6 2.8 fusion.17
  272.4 2.2 fusion.36
  274.6 2.8 fusion.16
  277.5 2.2 fusion.38
  279.7 3.0 fusion.15
  282.7 13.1 %fusion.23 = f32[2,4,128,256]{2,1,0,3:T(4,128)S(1)} fusion(bf16[2,4,128,256]{2,1,0,3:T(4,128)(2,1)S(1)} %reshape.164, f32[128,128,256,1]{1,0,3,2:T(8,128)S(1)} %copy-done.2, f32[2,1,128,256]{2,1,0,3:T(1,128)S(1)} %bitcast.85, f32[2,1,128,256]{2,1,0,3:T(1,128)S(1)} %bitcast.84, f32[2,1,128,256]{2,1,0,3:T(1,128)S(1)} %bitcast.83, ...), kind=kOutput, calls=%fused_computation.33 | convolution fusion | flops 403701760 | bytes 19398656 | tf_op jit(solution)/shard_map/tsc,bjsc->bjtc/dot_general | solution.py:67
  295.8 0.8 reshape.165
  296.7 8.1 %fusion.30 = bf16[2,512,256]{1,0,2:T(2,128)(2,1)S(1)} fusion(f32[2,512,256]{1,0,2:T(2,128)S(1)} %reshape.165, f32[512]{0:T(512)S(1)} %iota_convert_fusion, f32[16,256]{0,1:T(8,128)S(1)} %copy.66, f32[16,256]{0,1:T(8,128)S(1)} %copy.65, bf16[2,512,256]{1,0,2:T(2,128)(2,1)S(1)} %copy.67, f32[256]{0:T(256)S(1)} %dynamic_slice.37, ...), kind=kOutput, calls=%fused_computation.36 | convolution fusion | flops 55836672 | bytes 2395140 | tf_op jit(solution)/shard_map/ktc,kbc->btc/dot_general | solution.py:49
  304.8 1.0 copy.77
  305.8 23.6 %all_to_all.18 = bf16[2,512,256]{2,0,1:T(2,128)(2,1)S(1)} all-to-all(bf16[2,512,256]{2,0,1:T(2,128)(2,1)S(1)} %copy.77), channel_id=1, replica_groups=mesh['group'=1,'ctx'=32] {'ctx'}, dimensions={1} | all-to-all | bytes 1048576 | tf_op jit(solution)/shard_map/all_to_all | solution.py:85
  329.5 0.8 copy.86
  (122 shorter events, 7.0 us)
Async XLA Ops:
  6.5 25.4 %copy-start = (f32[16,8192]{1,0:T(8,128)S(1)}, f32[16,8192]{1,0:T(8,128)}, u32[]{:S(2)}) copy-start(f32[16,8192]{1,0:T(8,128)} %param.15) | copy-start | bytes 1572868
  6.5 257.6 %all-gather.2.cloned.1.call-start = ((), (), s32[]{:S(2)}) async-start(), calls=%async_computation.2 | async-start | bytes 8650752 | tf_op jit(solution)/shard_map/all_gather | solution.py:32
  7.3 289.4 %all-reduce.2.cloned.1.call-start = ((), (), s32[]{:S(2)}) async-start(), calls=%async_computation.1 | async-start | bytes 16777216 | tf_op jit(solution)/shard_map/psum | solution.py:30
  260.4 3.7 %copy-start.3 = (s32[2,512]{1,0:T(2,128)S(1)}, s32[2,512]{1,0:T(2,128)}, u32[]{:S(2)}) copy-start(s32[2,512]{1,0:T(2,128)} %param.13) | copy-start | bytes 12292
  269.6 13.2 %copy-start.2 = (f32[128,128,256,1]{1,0,3,2:T(8,128)S(1)}, f32[128,128,256,1]{1,0,3,2:T(8,128)}, u32[]{:S(2)}) copy-start(f32[128,128,256,1]{1,0,3,2:T(8,128)} %copy.80) | copy-start | bytes 50331652
  296.7 33.6 %copy-start.1 = (f32[16,8192]{1,0:T(8,128)S(1)}, f32[16,8192]{1,0:T(8,128)}, u32[]{:S(2)}) copy-start(f32[16,8192]{1,0:T(8,128)} %param.15) | copy-start | bytes 1572868
Sparse Core Ops, SparseCore 0:
  10.2 79.7 all-gather.1
  95.7 177.6 all-reduce.1
where the time goes:
time: 338 us; the launch traced here: 337 us
  other arithmetic  226 us (67%)
  matrix products  40.8 us (12%)
  local copies, waits for them, and re-layouts  31.4 us (9%)
  blocking collectives  23.6 us (7%)
  between operations  13.7 us (4%)
    add x16, other arithmetic, add_mode(): block + my_residue[index][None, None, :] * jnp.exp(-rate_row[None, None,...  196 us
    all_to_all x1, blocking collectives, body(): return lax.all_to_all(mixed, 'ctx', split_axis=1, concat_axis=2, tiled=True)  23.6 us
    select_n x1, local copies, waits for them, and re-layouts, body(): toeplitz = jnp.where(below, toeplitz, 0.0)  18.1 us
    select_n x1, other arithmetic, body(): toeplitz = jnp.where(below, toeplitz, 0.0)  13.4 us
    dot_general x1, matrix products, body(): jnp.einsum('tsc,bjsc->bjtc', toeplitz, pieces, precision=lax.Precision.HI...  13.1 us
    dot_general x4, matrix products, body(): jnp.einsum('kuc,kbc->buc', into_step, carry, precision=lax.Precision.HIGH...  11.5 us
    dot_general x1, matrix products, body(): jnp.einsum('ktc,kbc->btc', weighted, mine, precision=lax.Precision.HIGHEST)  8.11 us
    while x1, local copies, waits for them, and re-layouts, body(): partial_states = lax.map(per_mode, rates)  7.76 us
  transfers between devices with their start and end apart: 2, of which 0 were waited for; matrix products, arithmetic and copies ran while one was open for 85% of the time, Pallas kernels for 0%

commit v1 on v0

--- a/solution.py
+++ b/solution.py
@@ -1,9 +1,25 @@
+import functools
 import jax
 import jax.numpy as jnp
 from jax import lax
 from jax.sharding import PartitionSpec as P
 
 STEP_LEN = 128
+
+
+def _review_masks(frame_in, mesh_dim):
+    return jnp.concatenate(
+        lax.all_to_all(
+            jnp.stack(jnp.split(frame_in, lax.axis_size(mesh_dim), axis=1)),
+            axis_name=mesh_dim,
+            split_axis=0,
+            concat_axis=0,
+        ),
+        axis=2,
+    )
+
+
+store_positions = functools.partial(_review_masks, mesh_dim="ctx")
 
 
 def body(history, lengths, token_ids, embed, residue, decay, skip):
@@ -82,7 +98,7 @@
     far_part = jnp.stack(far_blocks, axis=1)
     conv_part = (near_part + far_part).reshape(seqs, generated, narrow)
     mixed = (history_part + conv_part + my_skip[None, None, :] * fresh_wide).astype(jnp.bfloat16)
-    return lax.all_to_all(mixed, "ctx", split_axis=1, concat_axis=2, tiled=True)
+    return store_positions(mixed)
 
 
 def solution(mesh):

time: 338 us -> 357 us (1.056)
  local copies, waits for them, and re-layouts: 31.4 us -> 50.3 us
    another operation x0 -> x35, local copies, waits for them, and re-layouts: none -> 19.8 us  [_review_masks(): jnp.stack(jnp.split(frame_in, lax.axis_size(mesh_dim), axis=1))]
  transfers between devices with their start and end apart: 2 -> 2, of which waited for: 0 -> 0; matrix products, arithmetic and copies ran while one was open for 85% -> 81% of each run, Pallas kernels for 0% -> 0%
where the time goes in v1:
time: 357 us; the launch traced here: 356 us
  other arithmetic  225 us (63%)
  local copies, waits for them, and re-layouts  50.3 us (14%)
  matrix products  40.7 us (11%)
  blocking collectives  24.3 us (7%)
  between operations  14 us (4%)
    add x16, other arithmetic, add_mode(): block + my_residue[index][None, None, :] * jnp.exp(-rate_row[None, None,...  195 us
    all_to_all x1, blocking collectives, _review_masks(): lax.all_to_all(jnp.stack(jnp.split(frame_in, lax.axis_size(mesh_dim), axi...  24.3 us
    another operation x35, local copies, waits for them, and re-layouts, _review_masks(): jnp.stack(jnp.split(frame_in, lax.axis_size(mesh_dim), axis=1))  19.8 us
    select_n x1, local copies, waits for them, and re-layouts, body(): toeplitz = jnp.where(below, toeplitz, 0.0)  18.2 us
    select_n x1, other arithmetic, body(): toeplitz = jnp.where(below, toeplitz, 0.0)  13.1 us
    dot_general x1, matrix products, body(): jnp.einsum('tsc,bjsc->bjtc', toeplitz, pieces, precision=lax.Precision.HI...  13.1 us
    dot_general x4, matrix products, body(): jnp.einsum('kuc,kbc->buc', into_step, carry, precision=lax.Precision.HIGH...  11.5 us
    dot_general x1, matrix products, body(): jnp.einsum('ktc,kbc->btc', weighted, mine, precision=lax.Precision.HIGHEST)  8.05 us
  transfers between devices with their start and end apart: 2, of which 0 were waited for; matrix products, arithmetic and copies ran while one was open for 81% of the time, Pallas kernels for 0%

profile of v1, /device:TPU:0, one launch (start us, length us, event | category | flops | bytes accessed | tf_op | source)
XLA Modules:
  0.0 356.2 jit_solution(10829059138405149583)
XLA Ops:
  6.5 0.7 all-gather.2.cloned.1.call-update
  7.3 1.1 broadcast_multiply_fusion
  8.4 0.7 broadcast_compare_fusion
  9.1 0.7 maximum_convert_fusion.1
  9.8 1.4 broadcast_select_fusion
  11.2 12.9 %while.25 = (s32[]{:T(128)}, f32[16,2,8192]{2,1,0:T(2,128)S(1)}, f32[16,8192]{1,0:T(8,128)S(1)}, bf16[2,32,8192]{2,1,0:T(8,128)(2,1)S(1)}, f32[2]{0:T(128)S(1)}, /*index=5*/s32[]{:T(128)}, s32[]{:T(128)}, s32[]{:T(128)}) while((s32[]{:T(128)}, f32[16,2,8192]{2,1,0:T(2,128)S(1)}, f32[16,8192]{1,0:T(8,128)S(1)}, ...), condition=%wide.region_2.3_spmd.clone, body=%wide.region_0.2_spmd.clone.sunk | while | flops 1859682 | bytes 3474285 | solution.py:45
  11.5 0.4 multiply_reduce_fusion.2
  12.3 0.4 multiply_reduce_fusion.2
  13.1 0.4 multiply_reduce_fusion.2
  13.9 0.4 multiply_reduce_fusion.2
  14.7 0.4 multiply_reduce_fusion.2
  15.5 0.4 multiply_reduce_fusion.2
  16.3 0.4 multiply_reduce_fusion.2
  18.7 0.4 multiply_reduce_fusion.2
  19.5 0.4 multiply_reduce_fusion.2
  20.3 0.4 multiply_reduce_fusion.2
  21.1 0.4 multiply_reduce_fusion.2
  23.5 0.4 multiply_reduce_fusion.2
  24.1 7.7 %copy.78 = f32[16,2,8192]{0,1,2:T(2,128)} copy(f32[16,2,8192]{2,1,0:T(2,128)S(1)} %get-tuple-element.131) | data formatting | bytes 2097152 | tf_op jit(solution)/shard_map/while | solution.py:45
  32.1 196.2 %while.26 = (s32[]{:T(128)}, f32[128,128,256]{2,1,0:T(8,128)}, f32[16,256]{1,0:T(8,128)S(1)}, f32[16,256]{1,0:T(8,128)S(1)}, s32[]{:T(128)}, /*index=5*/s32[]{:T(128)}) while((s32[]{:T(128)}, f32[128,128,256]{2,1,0:T(8,128)}, f32[16,256]{1,0:T(8,128)S(1)}, f32[16,256]{1,0:T(8,128)S(1)}, s32[]{:T(128)}, /*index=5*/s32[]{:T(128)}) %tuple.85), condition=%wide.region_5.6_spmd.clone, body=%wide.region_4.5_spmd.clone.sunk | while | flops 16826628 | bytes 33691736 | solution.py:79
  32.1 7.0 %select_add_fusion.2 = f32[128,128,256]{2,1,0:T(8,128)} fusion(f32[128,128,256]{2,1,0:T(8,128)} %get-tuple-element.310, f32[128,128]{1,0:T(8,128)S(1)} %maximum_convert_fusion.3, f32[256]{0:T(256)S(1)} %bitcast.148, f32[256]{0:T(256)S(1)} %bitcast.149, pred[]{:T(512)S(6)} %compare.3), kind=kLoop, calls=%fused_computation.8.clone.1 | loop fusion | flops 16777216 | bytes 33622016 | tf_op jit(solution)/shard_map/while/body/eval_jaxpr/add | solution.py:75
  39.2 12.4 %select_add_fusion.2 = f32[128,128,256]{2,1,0:T(8,128)} fusion(f32[128,128,256]{2,1,0:T(8,128)} %get-tuple-element.310, f32[128,128]{1,0:T(8,128)S(1)} %maximum_convert_fusion.3, f32[256]{0:T(256)S(1)} %bitcast.148, f32[256]{0:T(256)S(1)} %bitcast.149, pred[]{:T(512)S(6)} %compare.3), kind=kLoop, calls=%fused_computation.8.clone.1 | loop fusion | flops 16777216 | bytes 33622016 | tf_op jit(solution)/shard_map/while/body/eval_jaxpr/add | solution.py:75
  51.6 12.7 %select_add_fusion.2 = f32[128,128,256]{2,1,0:T(8,128)} fusion(f32[128,128,256]{2,1,0:T(8,128)} %get-tuple-element.310, f32[128,128]{1,0:T(8,128)S(1)} %maximum_convert_fusion.3, f32[256]{0:T(256)S(1)} %bitcast.148, f32[256]{0:T(256)S(1)} %bitcast.149, pred[]{:T(512)S(6)} %compare.3), kind=kLoop, calls=%fused_computation.8.clone.1 | loop fusion | flops 16777216 | bytes 33622016 | tf_op jit(solution)/shard_map/while/body/eval_jaxpr/add | solution.py:75
  64.4 12.5 %select_add_fusion.2 = f32[128,128,256]{2,1,0:T(8,128)} fusion(f32[128,128,256]{2,1,0:T(8,128)} %get-tuple-element.310, f32[128,128]{1,0:T(8,128)S(1)} %maximum_convert_fusion.3, f32[256]{0:T(256)S(1)} %bitcast.148, f32[256]{0:T(256)S(1)} %bitcast.149, pred[]{:T(512)S(6)} %compare.3), kind=kLoop, calls=%fused_computation.8.clone.1 | loop fusion | flops 16777216 | bytes 33622016 | tf_op jit(solution)/shard_map/while/body/eval_jaxpr/add | solution.py:75
  76.9 12.6 %select_add_fusion.2 = f32[128,128,256]{2,1,0:T(8,128)} fusion(f32[128,128,256]{2,1,0:T(8,128)} %get-tuple-element.310, f32[128,128]{1,0:T(8,128)S(1)} %maximum_convert_fusion.3, f32[256]{0:T(256)S(1)} %bitcast.148, f32[256]{0:T(256)S(1)} %bitcast.149, pred[]{:T(512)S(6)} %compare.3), kind=kLoop, calls=%fused_computation.8.clone.1 | loop fusion | flops 16777216 | bytes 33622016 | tf_op jit(solution)/shard_map/while/body/eval_jaxpr/add | solution.py:75
  89.6 13.0 %select_add_fusion.2 = f32[128,128,256]{2,1,0:T(8,128)} fusion(f32[128,128,256]{2,1,0:T(8,128)} %get-tuple-element.310, f32[128,128]{1,0:T(8,128)S(1)} %maximum_convert_fusion.3, f32[256]{0:T(256)S(1)} %bitcast.148, f32[256]{0:T(256)S(1)} %bitcast.149, pred[]{:T(512)S(6)} %compare.3), kind=kLoop, calls=%fused_computation.8.clone.1 | loop fusion | flops 16777216 | bytes 33622016 | tf_op jit(solution)/shard_map/while/body/eval_jaxpr/add | solution.py:75
  102.6 12.5 %select_add_fusion.2 = f32[128,128,256]{2,1,0:T(8,128)} fusion(f32[128,128,256]{2,1,0:T(8,128)} %get-tuple-element.310, f32[128,128]{1,0:T(8,128)S(1)} %maximum_convert_fusion.3, f32[256]{0:T(256)S(1)} %bitcast.148, f32[256]{0:T(256)S(1)} %bitcast.149, pred[]{:T(512)S(6)} %compare.3), kind=kLoop, calls=%fused_computation.8.clone.1 | loop fusion | flops 16777216 | bytes 33622016 | tf_op jit(solution)/shard_map/while/body/eval_jaxpr/add | solution.py:75
  115.2 12.6 %select_add_fusion.2 = f32[128,128,256]{2,1,0:T(8,128)} fusion(f32[128,128,256]{2,1,0:T(8,128)} %get-tuple-element.310, f32[128,128]{1,0:T(8,128)S(1)} %maximum_convert_fusion.3, f32[256]{0:T(256)S(1)} %bitcast.148, f32[256]{0:T(256)S(1)} %bitcast.149, pred[]{:T(512)S(6)} %compare.3), kind=kLoop, calls=%fused_computation.8.clone.1 | loop fusion | flops 16777216 | bytes 33622016 | tf_op jit(solution)/shard_map/while/body/eval_jaxpr/add | solution.py:75
  127.8 12.6 %select_add_fusion.2 = f32[128,128,256]{2,1,0:T(8,128)} fusion(f32[128,128,256]{2,1,0:T(8,128)} %get-tuple-element.310, f32[128,128]{1,0:T(8,128)S(1)} %maximum_convert_fusion.3, f32[256]{0:T(256)S(1)} %bitcast.148, f32[256]{0:T(256)S(1)} %bitcast.149, pred[]{:T(512)S(6)} %compare.3), kind=kLoop, calls=%fused_computation.8.clone.1 | loop fusion | flops 16777216 | bytes 33622016 | tf_op jit(solution)/shard_map/while/body/eval_jaxpr/add | solution.py:75
  140.5 12.5 %select_add_fusion.2 = f32[128,128,256]{2,1,0:T(8,128)} fusion(f32[128,128,256]{2,1,0:T(8,128)} %get-tuple-element.310, f32[128,128]{1,0:T(8,128)S(1)} %maximum_convert_fusion.3, f32[256]{0:T(256)S(1)} %bitcast.148, f32[256]{0:T(256)S(1)} %bitcast.149, pred[]{:T(512)S(6)} %compare.3), kind=kLoop, calls=%fused_computation.8.clone.1 | loop fusion | flops 16777216 | bytes 33622016 | tf_op jit(solution)/shard_map/while/body/eval_jaxpr/add | solution.py:75
  153.1 12.5 %select_add_fusion.2 = f32[128,128,256]{2,1,0:T(8,128)} fusion(f32[128,128,256]{2,1,0:T(8,128)} %get-tuple-element.310, f32[128,128]{1,0:T(8,128)S(1)} %maximum_convert_fusion.3, f32[256]{0:T(256)S(1)} %bitcast.148, f32[256]{0:T(256)S(1)} %bitcast.149, pred[]{:T(512)S(6)} %compare.3), kind=kLoop, calls=%fused_computation.8.clone.1 | loop fusion | flops 16777216 | bytes 33622016 | tf_op jit(solution)/shard_map/while/body/eval_jaxpr/add | solution.py:75
  165.6 12.4 %select_add_fusion.2 = f32[128,128,256]{2,1,0:T(8,128)} fusion(f32[128,128,256]{2,1,0:T(8,128)} %get-tuple-element.310, f32[128,128]{1,0:T(8,128)S(1)} %maximum_convert_fusion.3, f32[256]{0:T(256)S(1)} %bitcast.148, f32[256]{0:T(256)S(1)} %bitcast.149, pred[]{:T(512)S(6)} %compare.3), kind=kLoop, calls=%fused_computation.8.clone.1 | loop fusion | flops 16777216 | bytes 33622016 | tf_op jit(solution)/shard_map/while/body/eval_jaxpr/add | solution.py:75
  178.1 12.6 %select_add_fusion.2 = f32[128,128,256]{2,1,0:T(8,128)} fusion(f32[128,128,256]{2,1,0:T(8,128)} %get-tuple-element.310, f32[128,128]{1,0:T(8,128)S(1)} %maximum_convert_fusion.3, f32[256]{0:T(256)S(1)} %bitcast.148, f32[256]{0:T(256)S(1)} %bitcast.149, pred[]{:T(512)S(6)} %compare.3), kind=kLoop, calls=%fused_computation.8.clone.1 | loop fusion | flops 16777216 | bytes 33622016 | tf_op jit(solution)/shard_map/while/body/eval_jaxpr/add | solution.py:75
  190.7 12.4 %select_add_fusion.2 = f32[128,128,256]{2,1,0:T(8,128)} fusion(f32[128,128,256]{2,1,0:T(8,128)} %get-tuple-element.310, f32[128,128]{1,0:T(8,128)S(1)} %maximum_convert_fusion.3, f32[256]{0:T(256)S(1)} %bitcast.148, f32[256]{0:T(256)S(1)} %bitcast.149, pred[]{:T(512)S(6)} %compare.3), kind=kLoop, calls=%fused_computation.8.clone.1 | loop fusion | flops 16777216 | bytes 33622016 | tf_op jit(solution)/shard_map/while/body/eval_jaxpr/add | solution.py:75
  203.1 12.6 %select_add_fusion.2 = f32[128,128,256]{2,1,0:T(8,128)} fusion(f32[128,128,256]{2,1,0:T(8,128)} %get-tuple-element.310, f32[128,128]{1,0:T(8,128)S(1)} %maximum_convert_fusion.3, f32[256]{0:T(256)S(1)} %bitcast.148, f32[256]{0:T(256)S(1)} %bitcast.149, pred[]{:T(512)S(6)} %compare.3), kind=kLoop, calls=%fused_computation.8.clone.1 | loop fusion | flops 16777216 | bytes 33622016 | tf_op jit(solution)/shard_map/while/body/eval_jaxpr/add | solution.py:75
  215.8 12.4 %select_add_fusion.2 = f32[128,128,256]{2,1,0:T(8,128)} fusion(f32[128,128,256]{2,1,0:T(8,128)} %get-tuple-element.310, f32[128,128]{1,0:T(8,128)S(1)} %maximum_convert_fusion.3, f32[256]{0:T(256)S(1)} %bitcast.148, f32[256]{0:T(256)S(1)} %bitcast.149, pred[]{:T(512)S(6)} %compare.3), kind=kLoop, calls=%fused_computation.8.clone.1 | loop fusion | flops 16777216 | bytes 33622016 | tf_op jit(solution)/shard_map/while/body/eval_jaxpr/add | solution.py:75
  228.2 13.1 %select_bitcast_fusion = f32[128,128,256,1]{2,1,0,3:T(8,128)} fusion(f32[128,128,256]{2,1,0:T(8,128)} %get-tuple-element.132, pred[128,128]{1,0:T(8,128)(4,1)S(1)} %subtract_compare_fusion), kind=kLoop, calls=%fused_computation.12 | loop fusion | flops 4194304 | bytes 33570816 | tf_op jit(solution)/shard_map/jit(_where)/select_n | solution.py:82
  241.4 18.2 %copy.124 = f32[128,128,256,1]{1,0,3,2:T(8,128)} copy(f32[128,128,256,1]{2,1,0,3:T(8,128)} %select_bitcast_fusion) | data formatting | bytes 33554432 | tf_op jit(solution)/shard_map/jit(_where)/select_n | solution.py:82
  259.9 0.8 dynamic_slice.37
  260.7 2.8 fusion.18
  263.5 1.5 fusion.19
  265.0 0.5 copy.81
  265.9 0.6 fusion.65
  266.7 2.2 fusion.34
  268.9 2.8 fusion.17
  271.8 2.2 fusion.36
  274.0 2.8 fusion.16
  276.8 2.2 fusion.38
  279.0 3.0 fusion.15
  282.0 13.1 %fusion.23 = f32[2,4,128,256]{2,1,0,3:T(4,128)S(1)} fusion(bf16[2,4,128,256]{2,1,0,3:T(4,128)(2,1)S(1)} %reshape.170, f32[128,128,256,1]{1,0,3,2:T(8,128)S(1)} %copy-done.2, f32[2,1,128,256]{2,1,0,3:T(1,128)S(1)} %bitcast.147, f32[2,1,128,256]{2,1,0,3:T(1,128)S(1)} %bitcast.146, f32[2,1,128,256]{2,1,0,3:T(1,128)S(1)} %bitcast.145, ...), kind=kOutput, calls=%fused_computation.33 | convolution fusion | flops 403701760 | bytes 19398656 | tf_op jit(solution)/shard_map/tsc,bjsc->bjtc/dot_general | solution.py:83
  295.1 0.8 reshape.171
  296.0 8.0 %fusion.30 = bf16[2,512,256]{1,0,2:T(2,128)(2,1)S(1)} fusion(f32[2,512,256]{1,0,2:T(2,128)S(1)} %reshape.171, f32[512]{0:T(512)S(1)} %iota_convert_fusion, f32[16,256]{0,1:T(8,128)S(1)} %copy.80, f32[16,256]{0,1:T(8,128)S(1)} %copy.79, bf16[2,512,256]{1,0,2:T(2,128)(2,1)S(1)} %copy.81, f32[256]{0:T(256)S(1)} %dynamic_slice.37, ...), kind=kOutput, calls=%fused_computation.36 | convolution fusion | flops 55836672 | bytes 2395140 | tf_op jit(solution)/shard_map/ktc,kbc->btc/dot_general | solution.py:65
  304.0 2.5 slice_bitcast_fusion.19
  306.5 2.6 slice_bitcast_fusion
  309.2 1.6 copy.92
  310.8 1.6 copy.93
  312.4 1.6 copy.94
  314.0 1.6 copy.95
  315.6 1.6 copy.96
  317.1 1.6 copy.97
  318.7 1.6 copy.98
  320.3 1.6 copy.99
  324.3 24.3 %all_to_all.5 = bf16[32,2,16,256]{3,2,1,0:T(8,128)(2,1)S(1)} all-to-all(bf16[32,2,16,256]{3,2,1,0:T(8,128)(2,1)S(1)} %constant_dynamic-update-slice_fusion), channel_id=1, replica_groups=mesh['group'=1,'ctx'=32] {'ctx'}, dimensions={0} | all-to-all | bytes 1048576 | tf_op jit(solution)/shard_map/all_to_all | solution.py:12
  348.6 0.8 copy.130
  (202 shorter events, 11.7 us)
Async XLA Ops:
  6.5 25.4 %copy-start = (f32[16,8192]{1,0:T(8,128)S(1)}, f32[16,8192]{1,0:T(8,128)}, u32[]{:S(2)}) copy-start(f32[16,8192]{1,0:T(8,128)} %param.15) | copy-start | bytes 1572868
  6.5 257.0 %all-gather.2.cloned.1.call-start = ((), (), s32[]{:S(2)}) async-start(), calls=%async_computation.2 | async-start | bytes 8650752 | tf_op jit(solution)/shard_map/all_gather | solution.py:48
  7.3 288.7 %all-reduce.2.cloned.1.call-start = ((), (), s32[]{:S(2)}) async-start(), calls=%async_computation.1 | async-start | bytes 16777216 | tf_op jit(solution)/shard_map/psum | solution.py:46
  259.8 3.7 %copy-start.11 = (s32[2,512]{1,0:T(2,128)S(1)}, s32[2,512]{1,0:T(2,128)}, u32[]{:S(2)}) copy-start(s32[2,512]{1,0:T(2,128)} %param.13) | copy-start | bytes 12292
  268.9 13.1 %copy-start.2 = (f32[128,128,256,1]{1,0,3,2:T(8,128)S(1)}, f32[128,128,256,1]{1,0,3,2:T(8,128)}, u32[]{:S(2)}) copy-start(f32[128,128,256,1]{1,0,3,2:T(8,128)} %copy.124) | copy-start | bytes 50331652
  322.0 1.9 copy-start.9
  322.0 1.9 copy-start.8
  322.0 1.9 copy-start.7
  322.0 2.0 copy-start.6
  322.0 2.0 copy-start.5
  322.0 2.0 copy-start.4
  322.0 2.0 copy-start.3
  322.1 1.8 copy-start.10
  323.2 26.2 %copy-start.1 = (f32[16,8192]{1,0:T(8,128)S(1)}, f32[16,8192]{1,0:T(8,128)}, u32[]{:S(2)}) copy-start(f32[16,8192]{1,0:T(8,128)} %param.15) | copy-start | bytes 1572868
Sparse Core Ops, SparseCore 0:
  10.2 79.7 all-gather.1
  95.6 177.6 all-reduce.1
